TPU v7x, 128 devices: a whole 4x4x4 slice. The times are simulated.
128 devices in a mesh: rows: 16 (over x, z_hi, core), cols: 8 (over y, z_lo).
Axes of the slice: x: 4, y: 4, z: 4 (z_hi: 2, z_lo: 2; z = z_hi * 2 + z_lo), core: 2. Of those that a mesh axis runs over, the one named last changes fastest.
Arguments:
- values: float32 [256, 64, 32, 128], P(None, 'rows', 'cols'), may hold values from -6 to 6
- offsets: float32 [2, 64, 32, 128], P(None, 'rows', 'cols'), may hold values from 0 to 1
- nugget: float32 [64, 32, 128], P('rows', 'cols'), may hold values from 0.8 to 2.5
- neighbours: int32 [64, 32, 256], P('rows', 'cols'), may hold values from 0 to 262143, as said below
- length_scale: float32 [1], replicated, may hold values from 2.5 to 5
- target_tile: int32 [65536, 1], P(('rows', 'cols')), may hold values from 0 to 15; in each aligned block of 512 rows (0 to 511, 512 to 1023, ...) at most 64 rows name the same one
- target_spots: float32 [2, 65536], P(None, ('rows', 'cols')), may hold values from 0 to 1
Outputs:
- whitened: float32 [64, 32, 128, 256], P('rows', 'cols')
- cluster_terms: float32 [64, 32], P('rows', 'cols')
- predictions: float32 [65536, 256], P(('rows', 'cols'))
Inputs may be any that keep to these rules, and one draw needn't show every extreme that they name: `neighbours`: each cluster's 256 entries are distinct points of other clusters whose two grid coordinates each differ from the cluster's own by at most 2. `target_tile`: at most 64 of the 512 targets of one device name the same tile, and in every draw some tile is named exactly 64 times by the targets of some device.
All inputs are finite; a program needn't handle non-finite values.
Results may differ from a plain program's by a relative error of at most 0.0052.
Values may be sent and summed in bfloat16 or wider, within the bound.
No kernel may reach another device: no remote copies, remote signals or barrier semaphores. Data moves between devices by JAX's collectives and lax.ppermute only.
A program may use at most 256 MiB of HBM per device.

v0:
```python
import math

import jax
import jax.numpy as jnp
from jax import lax
from jax.sharding import PartitionSpec as P

HALO = 2


root_three = math.sqrt(3.0)


def extended_2(block, sides, width):
    for axis, dim in sides:
        count = lax.axis_size(axis)
        forward = [(i, i + 1) for i in range(count - 1)]
        backward = [(target, source) for source, target in forward]
        low = lax.ppermute(
            lax.slice_in_dim(block, block.shape[dim] - width, None, axis=dim), axis, forward
        )
        high = lax.ppermute(lax.slice_in_dim(block, 0, width, axis=dim), axis, backward)
        block = jnp.concatenate([low, block, high], axis=dim)
    return block


def matern(distances, length):
    scaled = root_three * distances / length
    return (1.0 + scaled) * jnp.exp(-scaled)


def cluster_work(point_data, reps, neigh, length):
    place_x = point_data[reps]
    place_y = point_data[reps + 1]
    noise_row = point_data[reps + 2]
    distances = jnp.sqrt(
        (place_x[:, None] - place_x[None, :]) ** 2 + (place_y[:, None] - place_y[None, :]) ** 2
    )
    covariance = matern(distances, length) + jnp.diag(noise_row)
    factor = jnp.linalg.cholesky(covariance)
    white_all = jax.scipy.linalg.solve_triangular(factor, point_data[:reps].T, lower=True)
    tail_rows = white_all[neigh:]
    log_diag = jnp.log(jnp.diagonal(factor)[neigh:])
    total_count = tail_rows.shape[0] * reps
    cluster_term = -(
        0.5 * jnp.sum(tail_rows * tail_rows) + reps * jnp.sum(log_diag)
    ) / total_count - 0.5 * math.log(2.0 * math.pi)
    return (tail_rows, cluster_term)


def cross_sum(target_x, target_y, point_x, point_y, weights, length, factor_scale):
    target_total = target_x.shape[0]
    point_total = point_x.shape[0]
    reps = weights.shape[1]
    target_step = math.gcd(target_total, 512)
    point_step = math.gcd(point_total, 4096)
    blocks_x = point_x.reshape(-1, point_step)
    blocks_y = point_y.reshape(-1, point_step)
    blocks_w = weights.reshape(-1, point_step, reps)

    def one_block(target_pair):
        rows_x, rows_y = target_pair

        def add_points(running, point_set):
            cols_x, cols_y, cols_w = point_set
            distances = jnp.sqrt(
                (rows_x[:, None] - cols_x[None, :]) ** 2 + (rows_y[:, None] - cols_y[None, :]) ** 2
            )
            kernel_bf = matern(distances, length).astype(jnp.bfloat16)
            return (running + jnp.dot(kernel_bf, cols_w, preferred_element_type=jnp.float32), None)

        summed, ignored = lax.scan(
            add_points, jnp.zeros((target_step, reps), jnp.float32), (blocks_x, blocks_y, blocks_w)
        )
        return summed * factor_scale

    mapped = lax.map(
        one_block, (target_x.reshape(-1, target_step), target_y.reshape(-1, target_step))
    )
    return mapped.reshape(target_total, reps)


def body(values, offsets, nugget, neighbours, length_scale, target_tile, target_spots):
    row_index = lax.axis_index("rows")
    col_index = lax.axis_index("cols")
    row_count = lax.axis_size("rows")
    col_count = lax.axis_size("cols")
    reps, span_x, span_y, block = values.shape
    neigh = neighbours.shape[2]
    grid_y = span_y * col_count
    length = length_scale[0]
    first_x = row_index * span_x
    first_y = col_index * span_y
    cell_x = (first_x + jnp.arange(span_x, dtype=jnp.int32)).astype(jnp.float32)
    cell_y = (first_y + jnp.arange(span_y, dtype=jnp.int32)).astype(jnp.float32)
    place_x = offsets[0] + cell_x[:, None, None]
    place_y = offsets[1] + cell_y[None, :, None]
    packed = jnp.concatenate([values, place_x[None], place_y[None], nugget[None]], axis=0)
    extended = extended_2(packed, (("rows", 1), ("cols", 2)), HALO)
    wide_y = span_y + 2 * HALO
    flat_table = extended.reshape(reps + 3, -1)
    grid_x_of = neighbours // (grid_y * block)
    grid_y_of = neighbours // block % grid_y
    member = neighbours % block
    remote_pos = (
        (grid_x_of - first_x + HALO) * wide_y + (grid_y_of - first_y + HALO)
    ) * block + member
    own_x = jnp.arange(span_x, dtype=jnp.int32)[:, None, None] + HALO
    own_y = jnp.arange(span_y, dtype=jnp.int32)[None, :, None] + HALO
    own_pos = (own_x * wide_y + own_y) * block + jnp.arange(block, dtype=jnp.int32)[None, None, :]
    cluster_total = span_x * span_y
    order_size = neigh + block
    all_pos = jnp.concatenate([remote_pos, own_pos], axis=2).reshape(cluster_total, order_size)
    picked = jnp.take(flat_table, all_pos, axis=1)
    group_size = math.gcd(cluster_total, 4)

    def run_cluster(point_data):
        return cluster_work(point_data, reps, neigh, length)

    def per_group(group_number):
        sliced = lax.dynamic_slice_in_dim(picked, group_number * group_size, group_size, 1)
        return jax.vmap(run_cluster, in_axes=1)(sliced)

    tails, terms = lax.map(per_group, jnp.arange(cluster_total // group_size, dtype=jnp.int32))
    weights = tails.reshape(-1, reps).astype(jnp.bfloat16)
    point_x = place_x.reshape(-1)
    point_y = place_y.reshape(-1)
    tgt_count = target_tile.shape[0]
    slots_per = 2 * tgt_count // row_count
    tile_ids = target_tile[:, 0]
    one_hot = (tile_ids[:, None] == jnp.arange(row_count, dtype=jnp.int32)[None, :]).astype(
        jnp.int32
    )
    rank_in_tile = jnp.sum((jnp.cumsum(one_hot, axis=0) - 1) * one_hot, axis=1)
    slot_index = tile_ids * slots_per + rank_in_tile
    send_x = jnp.zeros((row_count * slots_per,), jnp.float32).at[slot_index].set(target_spots[0])
    send_y = jnp.zeros((row_count * slots_per,), jnp.float32).at[slot_index].set(target_spots[1])
    outgoing = jnp.concatenate(
        [send_x.reshape(row_count, slots_per), send_y.reshape(row_count, slots_per)], axis=1
    )
    incoming = lax.all_to_all(outgoing, "rows", split_axis=0, concat_axis=0, tiled=True)
    spot_x = incoming[:, :slots_per].reshape(-1)
    spot_y = incoming[:, slots_per:].reshape(-1)
    target_x = (row_index.astype(jnp.float32) + spot_x) * span_x
    target_y = spot_y * grid_y
    inv_root = 1.0 / math.sqrt(span_x * grid_y * block)
    target_pairs = jnp.stack([target_x, target_y])
    gathered = lax.all_gather(target_pairs, "cols", axis=1, tiled=True)
    predicted = lax.psum_scatter(
        cross_sum(gathered[0], gathered[1], point_x, point_y, weights, length, inv_root),
        "cols",
        scatter_dimension=0,
        tiled=True,
    )
    returned = lax.all_to_all(
        predicted.reshape(row_count, slots_per, reps),
        "rows",
        split_axis=0,
        concat_axis=0,
        tiled=True,
    )
    predictions = returned.reshape(-1, reps)[slot_index]
    return (tails, terms, predictions)


def solution(mesh):
    return jax.shard_map(
        body,
        mesh=mesh,
        in_specs=(
            P(None, "rows", "cols", None),
            P(None, "rows", "cols", None),
            P("rows", "cols", None),
            P("rows", "cols", None),
            P(),
            P(("rows", "cols"), None),
            P(None, ("rows", "cols")),
        ),
        out_specs=(P("rows", "cols", None, None), P("rows", "cols"), P(("rows", "cols"), None)),
        check_vma=False,
    )
```

profile of v0, /device:TPU:1, one launch (start us, length us, event | category | flops | bytes accessed | tf_op | source)
XLA Modules:
  0.0 2253.3 jit_solution(2125543241801978611)
XLA Ops:
  27.3 40.7 %collective-permute-done = f32[259,2,4,128]{3,2,1,0:T(4,128)S(1)} collective-permute-done((f32[259,2,4,128]{3,2,1,0:T(4,128)}, f32[259,2,4,128]{3,2,1,0:T(4,128)S(1)}, u32[]{:S(2)}, u32[]{:S(2)}) %collective-permute-start) | collective-permute-done | bytes 1060896 | tf_op jit(solution)/shard_map/ppermute | solution.py:19
  93.4 52.2 %all-to-all-done = f32[16,1,128]{2,1,0:T(1,128)S(1)} async-done(((f32[16,1,128]{2,1,0:T(1,128)}), f32[16,1,128]{2,1,0:T(1,128)S(1)}, u32[]{:S(2)}, u32[]{:S(2)}) %all-to-all-start) | async-done | bytes 8224 | tf_op jit(solution)/shard_map/all_to_all | solution.py:141
  145.9 22.0 all_gather.3
  174.7 10.5 pad_maximum_fusion
  185.3 11.2 copy.89
  196.5 29.7 %gather_fusion.1 = f32[6144,259]{1,0:T(8,128)} fusion(f32[259,8192]{0,1:T(8,128)} %bitcast.150, s32[6144]{0:T(1024)S(1)} %broadcast_clamp_fusion), kind=kCustom, calls=%fused_computation.1 | custom fusion | bytes 12754944 | tf_op jit(solution)/shard_map/jit(_take)/gather | solution.py:114
  226.2 8.5 select_bitcast_fusion.2
  234.7 1732.7 %while.31 = (s32[]{:T(128)}, f32[4,4,128,256]{3,2,1,0:T(8,128)}, f32[4,4]{1,0:T(4,128)S(1)}, s32[4]{0:T(128)S(1)}, f32[259,16,384]{0,2,1:T(8,128)}, /*index=5*/f...) while((s32[]{:T(128)}, f32[4,4,128,256]{3,2,1,0:T(8,128)}, ...), condition=%wide.region_9.10_spmd, body=%wide.region_0.9_spmd.sunk | while | flops 1931693568 | bytes 58726568 | solution.py:124
  268.6 46.9 %custom-call.63 = f32[4,128,128]{2,1,0:T(8,128)S(1)} custom-call(f32[4,128,128]{2,1,0:T(8,128)S(1)} %cholesky.279), custom_call_target="Cholesky" | custom-call | tf_op jit(solution)/shard_map/while/body/eval_jaxpr/vmap(jit(cholesky))/cholesky | solution.py:40
  315.5 39.3 %custom-call.64 = f32[4,1,128,128]{2,3,1,0:T(8,128)S(1)} custom-call(f32[4,1,128,128]{3,2,1,0:T(8,128)S(1)} %select_bitcast_fusion.5), custom_call_target="InvertDiagBlocksLowerTriangular" | custom-call | tf_op jit(solution)/shard_map/while/body/eval_jaxpr/vmap(jit(cholesky))/cholesky | solution.py:40
  359.1 47.7 %custom-call.65 = f32[4,128,128]{2,1,0:T(8,128)S(1)} custom-call(f32[4,128,128]{2,1,0:T(8,128)} %cholesky.281), custom_call_target="Cholesky" | custom-call | tf_op jit(solution)/shard_map/while/body/eval_jaxpr/vmap(jit(cholesky))/cholesky | solution.py:40
  407.5 40.7 %custom-call.66 = f32[4,1,128,128]{2,3,1,0:T(8,128)} custom-call(f32[4,1,128,128]{3,2,1,0:T(8,128)} %get-tuple-element.370), custom_call_target="InvertDiagBlocksLowerTriangular" | custom-call | tf_op jit(solution)/shard_map/while/body/eval_jaxpr/vmap(jit(cholesky))/cholesky | solution.py:40
  451.2 46.9 %custom-call.67 = f32[4,128,128]{2,1,0:T(8,128)S(1)} custom-call(f32[4,128,128]{2,1,0:T(8,128)S(1)} %convolution_subtract_fusion.9), custom_call_target="Cholesky" | custom-call | tf_op jit(solution)/shard_map/while/body/eval_jaxpr/vmap(jit(cholesky))/cholesky | solution.py:40
  502.0 11.3 while.33
  513.3 118.7 %custom-call.69 = f32[4,3,128,128]{2,3,1,0:T(8,128)S(1)} custom-call(f32[4,3,128,128]{3,2,1,0:T(8,128)} %bitcast.177), custom_call_target="InvertDiagBlocksLowerTriangular" | custom-call | tf_op jit(solution)/shard_map/while/body/eval_jaxpr/vmap(jit(_solve_triangular))/triangular_solve | solution.py:41
  639.8 34.9 %copy.107 = f32[4,384,384]{0,2,1:T(8,128)} copy(f32[4,384,384]{2,1,0:T(8,128)S(1)} %copy-done) | data formatting | bytes 4718592 | tf_op jit(solution)/shard_map/while/body/eval_jaxpr/vmap(jit(cholesky))/select_n | solution.py:40
  674.8 8.3 gather_fusion
  696.5 46.9 %custom-call.63 = f32[4,128,128]{2,1,0:T(8,128)S(1)} custom-call(f32[4,128,128]{2,1,0:T(8,128)S(1)} %cholesky.279), custom_call_target="Cholesky" | custom-call | tf_op jit(solution)/shard_map/while/body/eval_jaxpr/vmap(jit(cholesky))/cholesky | solution.py:40
  743.5 39.3 %custom-call.64 = f32[4,1,128,128]{2,3,1,0:T(8,128)S(1)} custom-call(f32[4,1,128,128]{3,2,1,0:T(8,128)S(1)} %select_bitcast_fusion.5), custom_call_target="InvertDiagBlocksLowerTriangular" | custom-call | tf_op jit(solution)/shard_map/while/body/eval_jaxpr/vmap(jit(cholesky))/cholesky | solution.py:40
  787.0 47.7 %custom-call.65 = f32[4,128,128]{2,1,0:T(8,128)S(1)} custom-call(f32[4,128,128]{2,1,0:T(8,128)} %cholesky.281), custom_call_target="Cholesky" | custom-call | tf_op jit(solution)/shard_map/while/body/eval_jaxpr/vmap(jit(cholesky))/cholesky | solution.py:40
  835.5 40.7 %custom-call.66 = f32[4,1,128,128]{2,3,1,0:T(8,128)} custom-call(f32[4,1,128,128]{3,2,1,0:T(8,128)} %get-tuple-element.370), custom_call_target="InvertDiagBlocksLowerTriangular" | custom-call | tf_op jit(solution)/shard_map/while/body/eval_jaxpr/vmap(jit(cholesky))/cholesky | solution.py:40
  879.2 46.9 %custom-call.67 = f32[4,128,128]{2,1,0:T(8,128)S(1)} custom-call(f32[4,128,128]{2,1,0:T(8,128)S(1)} %convolution_subtract_fusion.9), custom_call_target="Cholesky" | custom-call | tf_op jit(solution)/shard_map/while/body/eval_jaxpr/vmap(jit(cholesky))/cholesky | solution.py:40
  930.0 11.3 while.33
  941.3 118.7 %custom-call.69 = f32[4,3,128,128]{2,3,1,0:T(8,128)S(1)} custom-call(f32[4,3,128,128]{3,2,1,0:T(8,128)} %bitcast.177), custom_call_target="InvertDiagBlocksLowerTriangular" | custom-call | tf_op jit(solution)/shard_map/while/body/eval_jaxpr/vmap(jit(_solve_triangular))/triangular_solve | solution.py:41
  1067.8 34.9 %copy.107 = f32[4,384,384]{0,2,1:T(8,128)} copy(f32[4,384,384]{2,1,0:T(8,128)S(1)} %copy-done) | data formatting | bytes 4718592 | tf_op jit(solution)/shard_map/while/body/eval_jaxpr/vmap(jit(cholesky))/select_n | solution.py:40
  1102.8 8.3 gather_fusion
  1124.8 46.9 %custom-call.63 = f32[4,128,128]{2,1,0:T(8,128)S(1)} custom-call(f32[4,128,128]{2,1,0:T(8,128)S(1)} %cholesky.279), custom_call_target="Cholesky" | custom-call | tf_op jit(solution)/shard_map/while/body/eval_jaxpr/vmap(jit(cholesky))/cholesky | solution.py:40
  1171.7 39.3 %custom-call.64 = f32[4,1,128,128]{2,3,1,0:T(8,128)S(1)} custom-call(f32[4,1,128,128]{3,2,1,0:T(8,128)S(1)} %select_bitcast_fusion.5), custom_call_target="InvertDiagBlocksLowerTriangular" | custom-call | tf_op jit(solution)/shard_map/while/body/eval_jaxpr/vmap(jit(cholesky))/cholesky | solution.py:40
  1215.3 47.7 %custom-call.65 = f32[4,128,128]{2,1,0:T(8,128)S(1)} custom-call(f32[4,128,128]{2,1,0:T(8,128)} %cholesky.281), custom_call_target="Cholesky" | custom-call | tf_op jit(solution)/shard_map/while/body/eval_jaxpr/vmap(jit(cholesky))/cholesky | solution.py:40
  1263.7 40.7 %custom-call.66 = f32[4,1,128,128]{2,3,1,0:T(8,128)} custom-call(f32[4,1,128,128]{3,2,1,0:T(8,128)} %get-tuple-element.370), custom_call_target="InvertDiagBlocksLowerTriangular" | custom-call | tf_op jit(solution)/shard_map/while/body/eval_jaxpr/vmap(jit(cholesky))/cholesky | solution.py:40
  1307.4 46.9 %custom-call.67 = f32[4,128,128]{2,1,0:T(8,128)S(1)} custom-call(f32[4,128,128]{2,1,0:T(8,128)S(1)} %convolution_subtract_fusion.9), custom_call_target="Cholesky" | custom-call | tf_op jit(solution)/shard_map/while/body/eval_jaxpr/vmap(jit(cholesky))/cholesky | solution.py:40
  1358.2 11.3 while.33
  1369.5 118.7 %custom-call.69 = f32[4,3,128,128]{2,3,1,0:T(8,128)S(1)} custom-call(f32[4,3,128,128]{3,2,1,0:T(8,128)} %bitcast.177), custom_call_target="InvertDiagBlocksLowerTriangular" | custom-call | tf_op jit(solution)/shard_map/while/body/eval_jaxpr/vmap(jit(_solve_triangular))/triangular_solve | solution.py:41
  1496.0 34.9 %copy.107 = f32[4,384,384]{0,2,1:T(8,128)} copy(f32[4,384,384]{2,1,0:T(8,128)S(1)} %copy-done) | data formatting | bytes 4718592 | tf_op jit(solution)/shard_map/while/body/eval_jaxpr/vmap(jit(cholesky))/select_n | solution.py:40
  1531.0 8.3 gather_fusion
  1552.6 46.9 %custom-call.63 = f32[4,128,128]{2,1,0:T(8,128)S(1)} custom-call(f32[4,128,128]{2,1,0:T(8,128)S(1)} %cholesky.279), custom_call_target="Cholesky" | custom-call | tf_op jit(solution)/shard_map/while/body/eval_jaxpr/vmap(jit(cholesky))/cholesky | solution.py:40
  1599.6 39.3 %custom-call.64 = f32[4,1,128,128]{2,3,1,0:T(8,128)S(1)} custom-call(f32[4,1,128,128]{3,2,1,0:T(8,128)S(1)} %select_bitcast_fusion.5), custom_call_target="InvertDiagBlocksLowerTriangular" | custom-call | tf_op jit(solution)/shard_map/while/body/eval_jaxpr/vmap(jit(cholesky))/cholesky | solution.py:40
  1643.1 47.7 %custom-call.65 = f32[4,128,128]{2,1,0:T(8,128)S(1)} custom-call(f32[4,128,128]{2,1,0:T(8,128)} %cholesky.281), custom_call_target="Cholesky" | custom-call | tf_op jit(solution)/shard_map/while/body/eval_jaxpr/vmap(jit(cholesky))/cholesky | solution.py:40
  1691.6 40.7 %custom-call.66 = f32[4,1,128,128]{2,3,1,0:T(8,128)} custom-call(f32[4,1,128,128]{3,2,1,0:T(8,128)} %get-tuple-element.370), custom_call_target="InvertDiagBlocksLowerTriangular" | custom-call | tf_op jit(solution)/shard_map/while/body/eval_jaxpr/vmap(jit(cholesky))/cholesky | solution.py:40
  1735.3 46.9 %custom-call.67 = f32[4,128,128]{2,1,0:T(8,128)S(1)} custom-call(f32[4,128,128]{2,1,0:T(8,128)S(1)} %convolution_subtract_fusion.9), custom_call_target="Cholesky" | custom-call | tf_op jit(solution)/shard_map/while/body/eval_jaxpr/vmap(jit(cholesky))/cholesky | solution.py:40
  1786.1 11.3 while.33
  1797.4 118.7 %custom-call.69 = f32[4,3,128,128]{2,3,1,0:T(8,128)S(1)} custom-call(f32[4,3,128,128]{3,2,1,0:T(8,128)} %bitcast.177), custom_call_target="InvertDiagBlocksLowerTriangular" | custom-call | tf_op jit(solution)/shard_map/while/body/eval_jaxpr/vmap(jit(_solve_triangular))/triangular_solve | solution.py:41
  1923.9 34.9 %copy.107 = f32[4,384,384]{0,2,1:T(8,128)} copy(f32[4,384,384]{2,1,0:T(8,128)S(1)} %copy-done) | data formatting | bytes 4718592 | tf_op jit(solution)/shard_map/while/body/eval_jaxpr/vmap(jit(cholesky))/select_n | solution.py:40
  1958.8 8.3 gather_fusion
  1969.2 78.5 %while.32 = (s32[]{:T(128)}, f32[16,512,256]{2,1,0:T(8,128)}, f32[16,512]{1,0:T(8,128)}, f32[1,2048]{1,0:T(1,128)S(1)}, f32[16,512]{1,0:T(8,128)}, /*index=5*/f3...) while((s32[]{:T(128)}, f32[16,512,256]{2,1,0:T(8,128)}, ...), condition=%wide.region_16.17_spmd, body=%wide.region_15.16_spmd.sunk | while | flops 548536320 | bytes 1602157 | solution.py:77
  2047.8 171.7 %reduce-scatter.2.cloned.1.call-done = f32[1024,256]{1,0:T(8,128)} async-done(((f32[8192,256]{1,0:T(8,128)}), f32[1024,256]{1,0:T(8,128)}) %reduce-scatter.2.cloned.1.call-update) | async-done | bytes 1048592 | tf_op jit(solution)/shard_map/reduce_scatter | solution.py:149
  2219.4 7.2 all-to-all-start.1
  2226.6 17.2 all-to-all-done.1
  (310 shorter events, 309.6 us)
Async XLA Ops:
  10.0 10.6 copy-start.4
  10.1 12.1 copy-start.10
  10.1 57.9 %copy-start.2 = (f32[256,4,4,128]{3,2,1,0:T(4,128)S(1)}, f32[256,4,4,128]{3,2,1,0:T(4,128)}, u32[]{:S(2)}) copy-start(f32[256,4,4,128]{3,2,1,0:T(4,128)} %param.11) | copy-start | bytes 6291460
  10.1 57.9 %copy-start.3 = (f32[4,4,128]{2,1,0:T(4,128)S(1)}, f32[4,4,128]{2,1,0:T(4,128)}, u32[]{:S(2)}) copy-start(f32[4,4,128]{2,1,0:T(4,128)} %param.13) | copy-start | bytes 24580
  11.8 56.2 %collective-permute-start = (f32[259,2,4,128]{3,2,1,0:T(4,128)}, f32[259,2,4,128]{3,2,1,0:T(4,128)S(1)}, u32[]{:S(2)}, u32[]{:S(2)}) collective-permute-start(f32[259,2,4,128]{3,2,1,0:T(4,128)} %get-tuple-element.219), channel_id=1, source_target_pairs={{0,8},{8,16},{16,24},{24,32},{32,40},{40,48},{48,56},{56,64},{64,7... | collective-permute-start | bytes 3182600 | tf_op jit(solution)/shard_map/ppermute | solution.py:19
  18.7 49.3 %collective-permute-start.1 = (f32[259,2,4,128]{3,2,1,0:T(4,128)}, f32[259,2,4,128]{3,2,1,0:T(4,128)}, u32[]{:S(2)}, u32[]{:S(2)}) collective-permute-start(f32[259,2,4,128]{3,2,1,0:T(4,128)} %get-tuple-element.220), channel_id=1, source_target_pairs={{8,0},{16,8},{24,16},{32,24},{40,32},{48,40},{56,48},{64,56},{72,6... | collective-permute-start | bytes 3182600 | tf_op jit(solution)/shard_map/ppermute | solution.py:22
  22.2 2.5 copy-start.8
  76.8 15.1 copy-start.5
  78.2 91.1 %collective-permute-start.3 = (f32[259,8,2,128]{3,1,2,0:T(8,128)}, f32[259,8,2,128]{3,1,2,0:T(8,128)}, u32[]{:S(2)}, u32[]{:S(2)}) collective-permute-start(f32[259,8,2,128]{3,1,2,0:T(8,128)} %copy.86), channel_id=1, source_target_pairs={{1,0},{2,1},{3,2},{4,3},{5,4},{6,5},{7,6},{9,8},{10,9},{11,10},{12... | collective-permute-start | bytes 6365192 | tf_op jit(solution)/shard_map/ppermute | solution.py:22
  79.5 92.5 %collective-permute-start.2 = (f32[259,8,2,128]{3,1,2,0:T(8,128)}, f32[259,8,2,128]{3,1,2,0:T(8,128)}, u32[]{:S(2)}, u32[]{:S(2)}) collective-permute-start(f32[259,8,2,128]{3,1,2,0:T(8,128)} %copy.85), channel_id=1, source_target_pairs={{0,1},{1,2},{2,3},{3,4},{4,5},{5,6},{6,7},{8,9},{9,10},{10,11},{11... | collective-permute-start | bytes 6365192 | tf_op jit(solution)/shard_map/ppermute | solution.py:19
  85.5 60.1 %all-to-all-start = ((f32[16,1,128]{2,1,0:T(1,128)}), f32[16,1,128]{2,1,0:T(1,128)S(1)}, u32[]{:S(2)}, u32[]{:S(2)}) async-start(f32[16,1,128]{2,1,0:T(1,128)} %bitcast.33), calls=%async_computation | async-start | bytes 16384 | tf_op jit(solution)/shard_map/all_to_all | solution.py:141
  91.7 2127.8 %reduce-scatter.2.cloned.1.call-start = ((), (), s32[]{:S(2)}) async-start(), calls=%async_computation.3 | async-start | bytes 9437184 | tf_op jit(solution)/shard_map/reduce_scatter | solution.py:149
  267.1 1.4 copy-start.1
  636.1 3.7 copy-start
  695.1 1.4 copy-start.1
  1064.1 3.7 copy-start
  1123.4 1.4 copy-start.1
  1492.3 3.7 copy-start
  1551.2 1.4 copy-start.1
  1920.2 3.7 copy-start
  1967.4 1.8 copy-start.11
  1967.4 1.8 copy-start.6
  1967.4 1.8 copy-start.7
  2047.7 178.9 %copy-start.9 = (s32[512,1]{0,1:T(1,128)S(1)}, s32[512,1]{0,1:T(1,128)}, u32[]{:S(2)}) copy-start(s32[512,1]{0,1:T(1,128)} %copy-done.8) | copy-start | bytes 6148
  2219.4 24.4 %all-to-all-start.1 = ((f32[16,64,256]{2,1,0:T(8,128)}), f32[16,64,256]{2,1,0:T(8,128)S(1)}, u32[]{:S(2)}, u32[]{:S(2)}) async-start(f32[16,64,256]{2,1,0:T(8,128)} %bitcast.155), calls=%async_computation.2 | async-start | bytes 2097152 | tf_op jit(solution)/shard_map/all_to_all | solution.py:155
Sparse Core Ops, SparseCore 0:
  2047.9 171.4 reduce-scatter.1
where the time goes:
time: 2260 us; the launch traced here: 2250 us
  other arithmetic  1430 us (63%)
  local copies, waits for them, and re-layouts  327 us (14%)
  waiting for transfers between devices  282 us (12%)
  matrix products  122 us (5%)
  starting transfers between devices  28.8 us (1%)
  loops' own time  24 us (1%)
    another operation x56, other arithmetic, cluster_work(): factor = jnp.linalg.cholesky(covariance)  891 us
    another operation x16, other arithmetic, cluster_work(): jax.scipy.linalg.solve_triangular(factor, point_data[:reps].T, lower=True)  492 us
    reduce_scatter x1, waiting for transfers between devices, body(): lax.psum_scatter(cross_sum(gathered[0], gathered[1], point_x, point_y, we...  172 us
    select_n x4, local copies, waits for them, and re-layouts, cluster_work(): factor = jnp.linalg.cholesky(covariance)  140 us
    dot_general x16, matrix products, add_points(): jnp.dot(kernel_bf, cols_w, preferred_element_type=jnp.float32)  66.6 us
    all_to_all x1, waiting for transfers between devices, body(): lax.all_to_all(outgoing, 'rows', split_axis=0, concat_axis=0, tiled=True)  52.2 us
    another operation x38, local copies, waits for them, and re-layouts  45.5 us
  transfers between devices with their start and end apart: 7, of which 4 were waited for; matrix products, arithmetic and copies ran while one was open for 1% of the time, Pallas kernels for 0%

commit v1 on v0

v1 whole, which is shorter than its diff:
```python
import math

import jax
import jax.numpy as jnp

from jax import lax
from jax.experimental import pallas as pl
from jax.experimental.pallas import tpu as pltpu
from jax.sharding import PartitionSpec as P

F32 = jnp.float32
BF = jnp.bfloat16
NN = (((1,), (0,)), ((), ()))
NT = (((1,), (1,)), ((), ()))
TN = (((0,), (0,)), ((), ()))


def split(x):
    hi = x.astype(BF)
    return hi, (x - hi.astype(F32)).astype(BF)


def dot(a, b, dims):
    return lax.dot_general(a, b, dims, preferred_element_type=F32)


def mm_nt(a, b):
    ah, al = split(a)
    bh, bl = split(b)
    return dot(jnp.concatenate([ah, ah, al], 1), jnp.concatenate([bh, bl, bh], 1), NT)


def mm_nn(a, b):
    ah, al = split(a)
    bh, bl = split(b)
    return dot(jnp.concatenate([ah, ah, al], 1), jnp.concatenate([bh, bl, bh], 0), NN)


def lane_take(x, idx):
    return jnp.take_along_axis(x, idx, axis=1, mode="promise_in_bounds")


def recip(p):
    r = pl.reciprocal(p, approx=True)
    return r * (2.0 - p * r)


def leaf_factor(leaf, lane, sub):
    base = lane & 96
    col = lane & 31
    x = [list(p) for p in leaf]
    piv = [[jnp.ones((8, 128), F32) for _ in range(4)] for _ in range(4)]
    for j in range(32):
        v0, s0 = divmod(j, 8)
        idx = base + j
        unit = jnp.where(col == j, 1.0, 0.0)
        below = sub > s0
        here = sub == s0
        for p in range(4):
            row = jnp.broadcast_to(x[p][v0][s0 : s0 + 1, :], (8, 128))
            d = lane_take(row, idx)
            r = recip(d)
            piv[p][v0] = jnp.where(here, d, piv[p][v0])
            rowp = row + unit
            for v in range(v0, 4):
                if v == v0 and s0 == 7:
                    continue
                c = lane_take(x[p][v], idx)
                if v == v0:
                    c = jnp.where(below, c, 0.0)
                x[p][v] = x[p][v] - (c * rowp) * r
    out = []
    for p in range(4):
        o = []
        for v in range(4):
            q = lax.rsqrt(piv[p][v])
            q = q * (1.5 - 0.5 * piv[p][v] * q * q)
            r_i = sub + 8 * v
            o.append(q * jnp.where(col < r_i, x[p][v], jnp.where(col == r_i, 1.0, 0.0)))
        out.append(o)
    return out


def inv_chol(xw, wp, count):
    lane8 = lax.broadcasted_iota(jnp.int32, (8, 128), 1)
    sub8 = lax.broadcasted_iota(jnp.int32, (8, 128), 0)
    lane = lax.broadcasted_iota(jnp.int32, (32, 128), 1)
    subl = lax.broadcasted_iota(jnp.int32, (32, 128), 0)
    for k in range(4):
        lo = 32 * k
        for base in range(0, count, 16):
            leaf = []
            for p in range(4):
                tiles = []
                for v in range(4):
                    acc = None
                    for g in range(4):
                        t = xw[base + 4 * p + g, lo + 8 * v : lo + 8 * v + 8, :]
                        t = pltpu.roll(t, (32 * (g - k)) % 128, axis=1) if g != k else t
                        acc = t if acc is None else jnp.where(lane8 // 32 == g, t, acc)
                    tiles.append(acc)
                leaf.append(tiles)
            inv = leaf_factor(leaf, lane8, sub8)
            for p in range(4):
                for v in range(4):
                    wp[p, 8 * v : 8 * v + 8, :] = inv[p][v]

            def apply(p, _):
                for g in range(4):
                    c = base + 4 * p + g
                    gi = 32 * g + (lane8 & 31)
                    wr = jnp.concatenate(
                        [lane_take(wp[p, 8 * v : 8 * v + 8, :], gi) for v in range(4)], 0
                    )
                    wh = wr.astype(BF).astype(F32)
                    lhs = jnp.where(lane < 64, wh, wr - wh).astype(BF)
                    r = xw[c, lo : lo + 32, :]
                    r = jnp.where(lane // 32 == k, jnp.where((lane & 31) == subl, 1.0, 0.0), r)
                    rh, rl = split(r)
                    t = dot(lhs, jnp.concatenate([rh, rl, rh, rl], 0), NN)
                    xw[c, lo : lo + 32, :] = jnp.where(lane < lo + 32, t, 0.0)
                    if k < 3:
                        th, tl = split(t)
                        u = dot(
                            jnp.concatenate([th, th, tl, tl], 0),
                            jnp.concatenate([th, tl, th, tl], 0),
                            TN,
                        )
                        n = 96 - lo
                        rest = xw[c, lo + 32 :, :]
                        ln = lax.broadcasted_iota(jnp.int32, (n, 128), 1)
                        xw[c, lo + 32 :, :] = jnp.where(ln // 32 == k, 0.0, rest) - u[lo + 32 :, :]
                return 0

            lax.fori_loop(0, 4, apply, 0)


def factor_kernel(first, length, nb, geo, gs, w3_out, xw, wp, cc, tt, l32s):
    count = 16
    lane8 = lax.broadcasted_iota(jnp.int32, (8, 128), 1)
    sub8 = lax.broadcasted_iota(jnp.int32, (8, 128), 0)
    scale = math.sqrt(3.0) / length[0]
    eye = (
        lax.broadcasted_iota(jnp.int32, (128, 128), 0)
        == lax.broadcasted_iota(jnp.int32, (128, 128), 1)
    )

    def window(c):
        ci, cj = c // 4, c % 4
        idx = nb[ci, pl.ds(cj, 1), :]
        gx = idx >> 12
        gy = (idx >> 7) & 31
        w = (gx - (first[0] + ci) + 2) * 5 + (gy - (first[1] + cj) + 2)
        return ci, cj, w, idx & 127

    def covariance(c, _):
        ci, cj, w, member = window(c)
        parts = []
        for h in range(2):
            wb = jnp.broadcast_to(w[:, 128 * h : 128 * h + 128], (8, 128))
            mb = jnp.broadcast_to(member[:, 128 * h : 128 * h + 128], (8, 128))
            acc = jnp.zeros((8, 128), F32)
            for wi in range(5):
                for wj in range(5):
                    if wi == 2 and wj == 2:
                        continue
                    shift = jnp.where(
                        sub8 == 0, float(wi - 2), jnp.where(sub8 == 1, float(wj - 2), 0.0)
                    )
                    t = lane_take(geo[ci + wi, cj + wj], mb) + shift
                    acc = jnp.where(wb == wi * 5 + wj, t, acc)
            parts.append(acc)
        parts.append(geo[ci + 2, cj + 2])
        pts = jnp.concatenate(parts, 1)
        cols = jnp.transpose(pts * scale)
        rows = pts * scale

        def block(a, b):
            dx = cols[128 * a : 128 * a + 128, 0:1] - rows[0:1, 128 * b : 128 * b + 128]
            dy = cols[128 * a : 128 * a + 128, 1:2] - rows[1:2, 128 * b : 128 * b + 128]
            s2 = dx * dx + dy * dy
            s = s2 * lax.rsqrt(jnp.maximum(s2, 1e-30))
            k = (1.0 + s) * jnp.exp(-s)
            if a == b:
                k = k + jnp.where(eye, pts[2:3, 128 * b : 128 * b + 128], 0.0)
            return k

        xw[c] = block(0, 0)
        cc[c, :128, :] = block(1, 0)
        cc[c, 128:, :] = block(2, 0)
        tt[c, :128, :128] = block(1, 1)
        tt[c, 128:, :128] = block(2, 1)
        tt[c, 128:, 128:] = block(2, 2)
        return 0

    lax.fori_loop(0, count, covariance, 0)
    inv_chol(xw, wp, count)

    def level1(q, _):
        for e in range(2):
            c = 2 * q + e
            w1 = xw[c]
            p = mm_nt(cc[c], w1)
            u = mm_nt(p, p)
            cc[c] = mm_nn(p, w1)
            xw[c] = tt[c, :128, :128] - u[:128, :128]
            tt[c, 128:, :128] = tt[c, 128:, :128] - u[128:, :128]
            tt[c, 128:, 128:] = tt[c, 128:, 128:] - u[128:, 128:]
        return 0

    lax.fori_loop(0, count // 2, level1, 0)
    inv_chol(xw, wp, count)

    def level2(q, _):
        for e in range(4):
            c = 4 * q + e
            w2 = xw[c]
            l32 = mm_nt(tt[c, 128:, :128], w2)
            l32s[c] = mm_nn(l32, w2)
            xw[c] = tt[c, 128:, 128:] - mm_nt(l32, l32)
        return 0

    lax.fori_loop(0, count // 4, level2, 0)
    inv_chol(xw, wp, count)

    def last(c, _):
        ci, cj, w, member = window(c)
        w3 = xw[c]
        w3_out[c] = w3
        q2 = l32s[c]
        q1 = cc[c, 128:, :] - mm_nn(q2, cc[c, :128, :])
        g = mm_nn(w3, jnp.concatenate([q1, q2], 1))
        gb = g.astype(BF).astype(F32)
        mb = jnp.broadcast_to(member, (128, 256))
        pick = jnp.where(lax.broadcasted_iota(jnp.int32, (128, 256), 0) == mb, 1.0, 0.0).astype(BF)
        for wi in range(5):
            lhs = jnp.concatenate(
                [jnp.where(w == wi * 5 + wj, gb, 0.0).astype(BF) for wj in range(5)], 0
            )
            s = dot(lhs, pick, NT).astype(BF)
            for wj in range(5):
                gs[c, wi, :, 128 * wj : 128 * wj + 128] = s[128 * wj : 128 * wj + 128, :]
        return 0

    lax.fori_loop(0, count, last, 0)


def factor(first, length, nb, geo):
    vm = pl.BlockSpec(memory_space=pltpu.VMEM)
    sm = pl.BlockSpec(memory_space=pltpu.SMEM)
    return pl.pallas_call(
        factor_kernel,
        out_shape=(
            jax.ShapeDtypeStruct((16, 5, 128, 640), BF),
            jax.ShapeDtypeStruct((16, 128, 128), F32),
        ),
        in_specs=[sm, sm, vm, vm],
        out_specs=(vm, vm),
        scratch_shapes=[
            pltpu.VMEM((16, 128, 128), F32),
            pltpu.VMEM((4, 32, 128), F32),
            pltpu.VMEM((16, 256, 128), F32),
            pltpu.VMEM((16, 256, 256), F32),
            pltpu.VMEM((16, 128, 128), F32),
        ],
        compiler_params=pltpu.CompilerParams(vmem_limit_bytes=60 << 20),
        name="factor",
    )(first, length, nb, geo)


def whiten_kernel(mid, north, south, west, east, nw, ne, sw, se, gs, w3, own, white, weights, term, tab):
    step = pl.program_id(0)

    @pl.when(step == 0)
    def _():
        tab[0:2, :, 0:256] = nw[...]
        tab[0:2, :, 256:768] = north[...]
        tab[0:2, :, 768:1024] = ne[...]
        tab[2:6, :, 0:256] = west[...]
        tab[2:6, :, 256:768] = mid[...]
        tab[2:6, :, 768:1024] = east[...]
        tab[6:8, :, 0:256] = sw[...]
        tab[6:8, :, 256:768] = south[...]
        tab[6:8, :, 768:1024] = se[...]

    ci, cj = step // 4, step % 4
    start = pl.multiple_of(cj * 128, 128)
    acc = mm_nt(w3[0], own[0])
    for wi in range(5):
        acc = acc - dot(gs[0, wi], tab[ci + wi, :, pl.ds(start, 640)], NT)
    white[0] = acc
    weights[...] = acc.astype(BF)
    eye = (
        lax.broadcasted_iota(jnp.int32, (128, 128), 0)
        == lax.broadcasted_iota(jnp.int32, (128, 128), 1)
    )
    diag = jnp.sum(jnp.where(eye, w3[0], 0.0), axis=0, keepdims=True)
    total = 0.5 * jnp.sum(acc * acc) - 256.0 * jnp.sum(jnp.log(diag))
    term[...] = jnp.full((1, 8, 128), -total / 32768.0 - 0.5 * math.log(2.0 * math.pi), F32)


def whiten(pieces, gs, w3, own):
    def whole(a):
        nd = a.ndim
        return pl.BlockSpec(a.shape, lambda s: (0,) * nd, pipeline_mode=pl.Buffered(1))

    return pl.pallas_call(
        whiten_kernel,
        grid=(16,),
        out_shape=(
            jax.ShapeDtypeStruct((16, 128, 256), F32),
            jax.ShapeDtypeStruct((2048, 256), BF),
            jax.ShapeDtypeStruct((16, 8, 128), F32),
        ),
        in_specs=[whole(p) for p in pieces]
        + [
            pl.BlockSpec((1, 5, 128, 640), lambda s: (s, 0, 0, 0)),
            pl.BlockSpec((1, 128, 128), lambda s: (s, 0, 0)),
            pl.BlockSpec((1, 256, 128), lambda s: (s // 4, 0, s % 4)),
        ],
        out_specs=(
            pl.BlockSpec((1, 128, 256), lambda s: (s, 0, 0)),
            pl.BlockSpec((128, 256), lambda s: (s, 0)),
            pl.BlockSpec((1, 8, 128), lambda s: (s, 0, 0)),
        ),
        scratch_shapes=[pltpu.VMEM((8, 256, 1024), BF)],
        compiler_params=pltpu.CompilerParams(vmem_limit_bytes=40 << 20),
        name="whiten",
    )(*pieces, gs, w3, own)


LN2 = math.log(2.0)
TB = 512


def pieces3(x):
    a = x.astype(BF).astype(F32)
    r = x - a
    b = r.astype(BF).astype(F32)
    return a, b, r - b


def cross_kernel(scale, tgt, pts, w, out, rhs):
    def form(x, y, left):
        q = x * x + y * y
        qs = pieces3(q)
        ones = jnp.ones_like(x)
        xs, ys = pieces3(x), pieces3(y)
        m = -2.0 if left else 1.0
        rows = []
        for a, b in ((0, 0), (0, 1), (1, 0), (0, 2), (1, 1), (2, 0)):
            k = a if left else b
            rows += [xs[k] * m, ys[k] * m]
        rows += (list(qs) + [ones] * 3) if left else ([ones] * 3 + list(qs))
        rows += [jnp.zeros_like(x)] * 14
        return jnp.concatenate(rows, 0).astype(BF)

    @pl.when(pl.program_id(0) == 0)
    def _():
        rhs[...] = form(pts[0:1, :] * scale[0], pts[1:2, :] * scale[0], False)

    lhs = form(tgt[0, 0:1, :] * scale[0], tgt[0, 1:2, :] * scale[0], True)
    acc = jnp.zeros((TB, 256), F32)
    for b in range(4):
        cut = slice(512 * b, 512 * b + 512)
        s2 = jnp.maximum(dot(lhs, rhs[:, cut], TN), 1e-30)
        s = s2 * lax.rsqrt(s2)
        k = (1.0 + s * LN2) * jnp.exp2(-s)
        acc = acc + dot(k.astype(BF), w[cut, :], NN)
    out[...] = (acc * scale[1]).astype(out.dtype)


def cross(scale, tgt, pts, w, dtype):
    n = tgt.shape[0]
    return pl.pallas_call(
        cross_kernel,
        grid=(n,),
        out_shape=jax.ShapeDtypeStruct((n * TB, 256), dtype),
        in_specs=[
            pl.BlockSpec(memory_space=pltpu.SMEM),
            pl.BlockSpec((1, 2, TB), lambda s: (s, 0, 0)),
            pl.BlockSpec((2, 2048), lambda s: (0, 0)),
            pl.BlockSpec((2048, 256), lambda s: (0, 0)),
        ],
        out_specs=pl.BlockSpec((TB, 256), lambda s: (s, 0)),
        scratch_shapes=[pltpu.VMEM((32, 2048), BF)],
        compiler_params=pltpu.CompilerParams(vmem_limit_bytes=40 << 20),
        name="cross",
    )(scale, tgt, pts, w)


def sum_kernel(parts, out):
    acc = parts[0].astype(F32)
    for i in range(1, 8):
        acc = acc + parts[i].astype(F32)
    out[...] = acc


def sum_parts(parts):
    n = parts.shape[1]
    return pl.pallas_call(
        sum_kernel,
        grid=(n // 256,),
        out_shape=jax.ShapeDtypeStruct((n, 256), F32),
        in_specs=[pl.BlockSpec((8, 256, 256), lambda s: (0, s, 0))],
        out_specs=pl.BlockSpec((256, 256), lambda s: (s, 0)),
        name="sum_parts",
    )(parts)


def shifted(x, dr, dc):
    pairs = [
        (r * 8 + c, (r + dr) * 8 + c + dc)
        for r in range(16)
        for c in range(8)
        if 0 <= r + dr < 16 and 0 <= c + dc < 8
    ]
    return lax.ppermute(x, ("rows", "cols"), pairs)


def surround(x, cut_r, cut_c):
    n = shifted(cut_r(x, 1), 1, 0)
    s = shifted(cut_r(x, 0), -1, 0)
    w = shifted(cut_c(x, 1), 0, 1)
    e = shifted(cut_c(x, 0), 0, -1)
    nw = shifted(cut_c(cut_r(x, 1), 1), 1, 1)
    ne = shifted(cut_c(cut_r(x, 1), 0), 1, -1)
    sw = shifted(cut_c(cut_r(x, 0), 1), -1, 1)
    se = shifted(cut_c(cut_r(x, 0), 0), -1, -1)
    return n, s, w, e, nw, ne, sw, se


def spread(x):
    return [x] + [
        lax.ppermute(x, "cols", [(i, (i + k) % 8) for i in range(8)]) for k in range(1, 8)
    ]


def body(values, offsets, nugget, neighbours, length_scale, target_tile, target_spots):
    row = lax.axis_index("rows")
    col = lax.axis_index("cols")
    length = length_scale[0]
    first = jnp.stack([row * 4, col * 4]).astype(jnp.int32)

    geo = jnp.concatenate(
        [offsets.transpose(1, 2, 0, 3), nugget[:, :, None, :], jnp.zeros((4, 4, 5, 128), F32)], 2
    )
    n, s, w, e, nw, ne, sw, se = surround(
        geo, lambda a, h: a[2 * h : 2 * h + 2], lambda a, h: a[:, 2 * h : 2 * h + 2]
    )
    geo_all = jnp.concatenate(
        [
            jnp.concatenate([nw, n, ne], 1),
            jnp.concatenate([w, geo, e], 1),
            jnp.concatenate([sw, s, se], 1),
        ],
        0,
    )

    own = values.transpose(1, 0, 2, 3).reshape(4, 256, 512)
    mid = own.astype(BF)
    around = surround(
        mid, lambda a, h: a[2 * h : 2 * h + 2], lambda a, h: a[:, :, 256 * h : 256 * h + 256]
    )

    tile_ids = target_tile[:, 0]
    one_hot = (tile_ids[:, None] == jnp.arange(16, dtype=jnp.int32)[None, :]).astype(jnp.int32)
    rank = jnp.sum((jnp.cumsum(one_hot, axis=0) - 1) * one_hot, axis=1)
    slot = tile_ids * 64 + rank
    send_x = jnp.zeros((1024,), F32).at[slot].set(target_spots[0])
    send_y = jnp.zeros((1024,), F32).at[slot].set(target_spots[1])
    outgoing = jnp.concatenate([send_x.reshape(16, 64), send_y.reshape(16, 64)], axis=1)
    incoming = lax.all_to_all(outgoing, "rows", split_axis=0, concat_axis=0, tiled=True)
    tx = incoming[:, :64].reshape(1024) * 4.0 - 2.0
    ty = incoming[:, 64:].reshape(1024) * 32.0
    spots = spread(jnp.stack([tx, ty]))
    spots = jnp.stack(spots)
    order = (col - jnp.arange(8, dtype=jnp.int32)) % 8
    spots = jnp.take(spots, order, axis=0)
    mid_y = (col * 4 + 2).astype(F32)
    tgt = jnp.stack([spots[:, 0], spots[:, 1] - mid_y], 1)
    tgt = tgt.reshape(8, 2, 1024 // TB, TB).transpose(0, 2, 1, 3).reshape(-1, 2, TB)

    gs, w3 = factor(first, length_scale, neighbours, geo_all)
    white, weights, term = whiten([mid, *around], gs, w3, own)

    px = offsets[0] + (jnp.arange(4, dtype=F32) - 2.0)[:, None, None]
    py = offsets[1] + (jnp.arange(4, dtype=F32) - 2.0)[None, :, None]
    pts = jnp.stack([px.reshape(-1), py.reshape(-1)])
    scale = jnp.stack([math.sqrt(3.0) / LN2 / length, jnp.float32(1.0 / 128.0)])
    partial = cross(scale, tgt, pts, weights, BF)
    shared = lax.all_to_all(
        partial.reshape(8, 1024, 256), "cols", split_axis=0, concat_axis=0, tiled=True
    )
    predicted = sum_parts(shared)
    returned = lax.all_to_all(
        predicted.reshape(16, 64, 256), "rows", split_axis=0, concat_axis=0, tiled=True
    )
    predictions = returned.reshape(-1, 256)[slot]
    return (white.reshape(4, 4, 128, 256), term[:, 0, 0].reshape(4, 4), predictions)


def solution(mesh):
    return jax.shard_map(
        body,
        mesh=mesh,
        in_specs=(
            P(None, "rows", "cols", None),
            P(None, "rows", "cols", None),
            P("rows", "cols", None),
            P("rows", "cols", None),
            P(),
            P(("rows", "cols"), None),
            P(None, ("rows", "cols")),
        ),
        out_specs=(P("rows", "cols", None, None), P("rows", "cols"), P(("rows", "cols"), None)),
        check_vma=False,
    )
```

time: 2260 us -> 361 us (0.16)
  other arithmetic: 1430 us -> 8.4 us
  local copies, waits for them, and re-layouts: 327 us -> 28.5 us
  waiting for transfers between devices: 282 us -> 33.2 us
  Pallas kernels: 0 us -> 150 us
  matrix products: 122 us -> 0 us
  starting transfers between devices: 28.8 us -> 82 us
  blocking collectives: 22 us -> 56.2 us
  loops' own time: 24 us -> 0 us
    another operation x76 -> x7, other arithmetic: 1380 us -> 2.56 us  [the longest x56 891 us: cluster_work(): factor = jnp.linalg.cholesky(covariance)]
    reduce_scatter x1 -> x0, waiting for transfers between devices: 172 us -> none  [body(): lax.psum_scatter(cross_sum(gathered[0], gathered[1], point_x, point_y, we...]
    pallas_call x0 -> x4, Pallas kernels: none -> 150 us  [the longest x1 92.2 us: factor(): pl.pallas_call(factor_kernel, out_shape=(jax.ShapeDtypeStruct((16, 5, 128...]
    select_n x5 -> x0, local copies, waits for them, and re-layouts: 140 us -> none  [the longest x4 140 us: cluster_work(): factor = jnp.linalg.cholesky(covariance)]
    dot_general x16 -> x0, matrix products: 66.6 us -> none  [add_points(): jnp.dot(kernel_bf, cols_w, preferred_element_type=jnp.float32)]
    gather x6 -> x2, local copies, waits for them, and re-layouts: 65.1 us -> 3.81 us  [the longest x1 2.23 us: body(): predictions = returned.reshape(-1, 256)[slot]]
    all_to_all x0 -> x1, blocking collectives: none -> 56.2 us  [body(): lax.all_to_all(partial.reshape(8, 1024, 256), 'cols', split_axis=0, conca...]
    another operation x36 -> x0, matrix products: 55.5 us -> none  [the longest x20 30.4 us: cluster_work(): jax.scipy.linalg.solve_triangular(factor, point_data[:reps].T, lower=True)]
  transfers between devices with their start and end apart: 7 -> 25, of which waited for: 4 -> 8; matrix products, arithmetic and copies ran while one was open for 1% -> 8% of each run, Pallas kernels for 0% -> 26%
where the time goes in v1:
time: 361 us; the launch traced here: 360 us
  Pallas kernels  150 us (42%)
  starting transfers between devices  82 us (23%)
  blocking collectives  56.2 us (16%)
  waiting for transfers between devices  33.2 us (9%)
  local copies, waits for them, and re-layouts  28.5 us (8%)
  other arithmetic  8.4 us (2%)
    pallas_call x1, Pallas kernels, factor(): pl.pallas_call(factor_kernel, out_shape=(jax.ShapeDtypeStruct((16, 5, 128...  92.2 us
    all_to_all x1, blocking collectives, body(): lax.all_to_all(partial.reshape(8, 1024, 256), 'cols', split_axis=0, conca...  56.2 us
    ppermute x16, starting transfers between devices, shifted(): return lax.ppermute(x, ('rows', 'cols'), pairs)  55.3 us
    pallas_call x1, Pallas kernels, cross(): pl.pallas_call(cross_kernel, grid=(n,), out_shape=jax.ShapeDtypeStruct((n...  33.8 us
    pallas_call x1, Pallas kernels, whiten(): pl.pallas_call(whiten_kernel, grid=(16,), out_shape=(jax.ShapeDtypeStruct...  19.3 us
    ppermute x7, waiting for transfers between devices, spread(): lax.ppermute(x, 'cols', [(i, (i + k) % 8) for i in range(8)])  16.9 us
    all_to_all x1, waiting for transfers between devices, body(): lax.all_to_all(predicted.reshape(16, 64, 256), 'rows', split_axis=0, conc...  16.3 us
    all_to_all x1, starting transfers between devices, body(): lax.all_to_all(predicted.reshape(16, 64, 256), 'rows', split_axis=0, conc...  10.8 us
  transfers between devices with their start and end apart: 25, of which 8 were waited for; matrix products, arithmetic and copies ran while one was open for 8% of the time, Pallas kernels for 26%

profile of v1, /device:TPU:1, one launch (start us, length us, event | category | flops | bytes accessed | tf_op | source)
XLA Modules:
  0.0 359.7 jit_solution(12805865164702679020)
XLA Ops:
  0.6 2.5 reshape.227
  3.7 1.0 fusion.13
  4.7 7.1 %collective-permute-start.4 = (bf16[2,256,256]{2,1,0:T(8,128)(2,1)}, bf16[2,256,256]{2,1,0:T(8,128)(2,1)S(1)}, u32[]{:S(2)}, u32[]{:S(2)}) collective-permute-start(bf16[2,256,256]{2,1,0:T(8,128)(2,1)} %get-tuple-element.16), channel_id=1, source_target_pairs={{0,9},{1,10},{2,11},{3,12},{4,13},{5,14},{6,15},{8,17},{9,18},{10,... | collective-permute-start | bytes 786440 | tf_op jit(solution)/shard_map/ppermute | solution.py:418
  12.5 1.3 collective-permute-start.15
  13.8 1.3 collective-permute-start.13
  15.1 1.3 collective-permute-start.10
  16.5 1.2 reduce-window.6
  18.0 2.4 scatter_custom_fusion.1
  20.5 2.4 scatter_custom_fusion
  23.7 9.5 %all-to-all-start = ((f32[16,1,128]{2,1,0:T(1,128)}), f32[16,1,128]{2,1,0:T(1,128)S(1)}, u32[]{:S(2)}, u32[]{:S(2)}) async-start(f32[16,1,128]{2,1,0:T(1,128)} %bitcast.13), calls=%async_computation | async-start | bytes 16384 | tf_op jit(solution)/shard_map/all_to_all | solution.py:473
  33.2 1.0 fusion.15
  34.3 1.0 fusion.14
  40.0 2.3 copy.18.own
  42.5 2.2 collective-permute-start.16
  45.3 3.4 collective-permute-done.16
  49.8 2.6 collective-permute-done.17
  53.0 4.3 %collective-permute-done.18 = f32[2,1024]{1,0:T(2,128)S(1)} collective-permute-done((f32[2,1024]{1,0:T(2,128)S(1)}, f32[2,1024]{1,0:T(2,128)S(1)}, u32[]{:S(2)}, u32[]{:S(2)}) %collective-permute-start.18) | collective-permute-done | bytes 8224 | tf_op jit(solution)/shard_map/ppermute | solution.py:435
  57.3 0.9 collective-permute-start.19
  58.9 2.5 collective-permute-done.19
  62.0 3.1 collective-permute-done.20
  65.1 1.6 collective-permute-start.21
  67.6 1.2 collective-permute-start.22
  70.1 1.3 collective-permute-start.5
  71.4 9.7 %collective-permute-start.14 = (f32[2,4,8,128]{3,2,1,0:T(8,128)}, f32[2,4,8,128]{3,2,1,0:T(8,128)}, u32[]{:S(2)}, u32[]{:S(2)}) collective-permute-start(f32[2,4,8,128]{3,2,1,0:T(8,128)} %get-tuple-element.28), channel_id=1, source_target_pairs={{8,0},{9,1},{10,2},{11,3},{12,4},{13,5},{14,6},{15,7},{16,8},{17,9... | collective-permute-start | bytes 98312 | tf_op jit(solution)/shard_map/ppermute | solution.py:418
  81.1 1.3 collective-permute-start.12
  82.4 9.5 %collective-permute-start.8 = (f32[2,2,8,128]{3,2,1,0:T(8,128)}, f32[2,2,8,128]{3,2,1,0:T(8,128)}, u32[]{:S(2)}, u32[]{:S(2)}) collective-permute-start(f32[2,2,8,128]{3,2,1,0:T(8,128)} %get-tuple-element.23), channel_id=1, source_target_pairs={{0,9},{1,10},{2,11},{3,12},{4,13},{5,14},{6,15},{8,17},{9,18},{10,... | collective-permute-start | bytes 49160 | tf_op jit(solution)/shard_map/ppermute | solution.py:418
  92.5 1.6 gather_fusion
  94.1 2.2 collective-permute-start.6
  96.4 3.3 collective-permute-start.11
  99.7 6.3 %collective-permute-start.9 = (f32[2,4,8,128]{3,2,1,0:T(8,128)}, f32[2,4,8,128]{3,2,1,0:T(8,128)S(1)}, u32[]{:S(2)}, u32[]{:S(2)}) collective-permute-start(f32[2,4,8,128]{3,2,1,0:T(8,128)} %get-tuple-element.27), channel_id=1, source_target_pairs={{0,8},{1,9},{2,10},{3,11},{4,12},{5,13},{6,14},{7,15},{8,16},{9,17... | collective-permute-start | bytes 98312 | tf_op jit(solution)/shard_map/ppermute | solution.py:418
  106.1 0.8 broadcast_select_fusion
  106.9 1.9 collective-permute-start
  108.8 3.2 collective-permute-start.1
  112.0 2.8 collective-permute-start.2
  114.8 1.3 collective-permute-start.3
  116.9 1.5 collective-permute-start.7
  119.1 0.9 reshape.191.tgt
  120.0 1.6 maximum_maximum_fusion.geo
  121.6 92.2 %factor.1 = (bf16[16,5,128,640]{3,2,1,0:T(8,128)(2,1)}, f32[16,128,128]{2,1,0:T(8,128)}) custom-call(s32[2]{0:T(128)} %pad_add_fusion.first, f32[1]{0:T(128)S(6)} %copy.32.length, s32[4,4,256]{2,1,0:T(4,128)} %nb.1, f32[8,8,8,128]{3,2,1,0:T(8,128)} %maximum_maximum_fusion.geo), custom_call_target="tpu_custom_call" | custom-call | tf_op jit(solution)/shard_map/factor/pallas_call | solution.py:251
  213.8 1.2 copy-done
  215.1 0.9 copy-done.2
  216.0 19.3 %whiten.1 = (f32[16,128,256]{2,1,0:T(8,128)}, bf16[2048,256]{1,0:T(8,128)(2,1)S(1)}, f32[16,8,128]{2,1,0:T(8,128)S(1)}) custom-call(bf16[4,256,512]{2,1,0:T(8,128)(2,1)S(1)} %copy.23.mid, bf16[2,256,512]{2,1,0:T(8,128)(2,1)} %collective-permute-done.north, bf16[2,256,512]{2,1,0:T(8,128)(2,1)} %collective-permute-done.1.south, ...), custom_call_target="tpu_custom_call" | custom-call | tf_op jit(solution)/shard_map/whiten/pallas_call | solution.py:307
  235.3 33.8 %cross.1 = bf16[8192,256]{1,0:T(8,128)(2,1)S(1)} custom-call(f32[2]{0:T(128)S(1)} %copy-done.3, f32[16,2,512]{2,1,0:T(2,128)S(1)} %reshape.191.tgt, f32[2,2048]{1,0:T(2,128)S(1)} %pad_maximum_fusion.2.pts, bf16[2048,256]{1,0:T(8,128)(2,1)S(1)} %get-tuple-element.12.w), custom_call_target="tpu_custom_call" | custom-call | tf_op jit(solution)/shard_map/cross/pallas_call | solution.py:375
  269.1 56.2 %all_to_all.22.parts = bf16[8,1024,256]{2,1,0:T(8,128)(2,1)} all-to-all(bf16[8,1024,256]{2,1,0:T(8,128)(2,1)S(1)} %bitcast.58), channel_id=1, replica_groups=mesh['rows'=16,'cols'=8] {'cols'}, dimensions={0} | all-to-all | bytes 8388608 | tf_op jit(solution)/shard_map/all_to_all | solution.py:492
  325.3 4.2 %sum_parts.1 = f32[1024,256]{1,0:T(8,128)} custom-call(bf16[8,1024,256]{2,1,0:T(8,128)(2,1)} %all_to_all.22.parts), custom_call_target="tpu_custom_call" | custom-call | tf_op jit(solution)/shard_map/sum_parts/pallas_call | solution.py:401
  329.5 10.8 %all-to-all-start.2 = ((f32[16,64,256]{2,1,0:T(8,128)}), f32[16,64,256]{2,1,0:T(8,128)S(1)}, u32[]{:S(2)}, u32[]{:S(2)}) async-start(f32[16,64,256]{2,1,0:T(8,128)} %bitcast.60), calls=%async_computation.2 | async-start | bytes 2097152 | tf_op jit(solution)/shard_map/all_to_all | solution.py:496
  341.2 16.3 %all-to-all-done.2 = f32[16,64,256]{2,1,0:T(8,128)S(1)} async-done(((f32[16,64,256]{2,1,0:T(8,128)}), f32[16,64,256]{2,1,0:T(8,128)S(1)}, u32[]{:S(2)}, u32[]{:S(2)}) %all-to-all-start.2) | async-done | bytes 1048608 | tf_op jit(solution)/shard_map/all_to_all | solution.py:496
  357.5 2.2 gather_fusion.1
  (99 shorter events, 15.4 us)
Async XLA Ops:
  3.1 1.7 copy-start.4
  3.1 8.7 %copy-start.6 = (f32[2,4,4,128]{3,2,1,0:T(4,128)S(1)}, f32[2,4,4,128]{3,2,1,0:T(4,128)}, u32[]{:S(2)}) copy-start(f32[2,4,4,128]{3,2,1,0:T(4,128)} %param.8) | copy-start | bytes 49156
  3.1 8.7 %copy-start.7 = (f32[4,4,128]{2,1,0:T(4,128)S(1)}, f32[4,4,128]{2,1,0:T(4,128)}, u32[]{:S(2)}) copy-start(f32[4,4,128]{2,1,0:T(4,128)} %param.9) | copy-start | bytes 24580
  3.1 13.3 %copy-start.10 = (s32[512,1]{0,1:T(1,128)S(1)}, s32[512,1]{0,1:T(1,128)}, u32[]{:S(2)}) copy-start(s32[512,1]{0,1:T(1,128)} %param.12) | copy-start | bytes 6148
  3.7 14.3 %copy-start.15 = (f32[2,512]{1,0:T(2,128)S(1)}, f32[2,512]{1,0:T(2,128)}, u32[]{:S(2)}) copy-start(f32[2,512]{1,0:T(2,128)} %param.13) | copy-start | bytes 12292
  4.7 107.3 %collective-permute-start.4 = (bf16[2,256,256]{2,1,0:T(8,128)(2,1)}, bf16[2,256,256]{2,1,0:T(8,128)(2,1)S(1)}, u32[]{:S(2)}, u32[]{:S(2)}) collective-permute-start(bf16[2,256,256]{2,1,0:T(8,128)(2,1)} %get-tuple-element.16), channel_id=1, source_target_pairs={{0,9},{1,10},{2,11},{3,12},{4,13},{5,14},{6,15},{8,17},{9,18},{10,... | collective-permute-start | bytes 786440 | tf_op jit(solution)/shard_map/ppermute | solution.py:418
  11.8 4.6 %copy-start.5 = (f32[2,4,4,128]{3,0,2,1:T(2,128)}, f32[2,4,4,128]{3,0,2,1:T(2,128)S(1)}, u32[]{:S(2)}) copy-start(f32[2,4,4,128]{3,0,2,1:T(2,128)S(1)} %copy.24) | copy-start | bytes 49156
  12.5 58.8 %collective-permute-start.15 = (f32[2,2,8,128]{3,2,1,0:T(8,128)}, f32[2,2,8,128]{3,2,1,0:T(8,128)S(1)}, u32[]{:S(2)}, u32[]{:S(2)}) collective-permute-start(f32[2,2,8,128]{3,2,1,0:T(8,128)} %get-tuple-element.25), channel_id=1, source_target_pairs={{9,0},{10,1},{11,2},{12,3},{13,4},{14,5},{15,6},{17,8},{18,9},{19,... | collective-permute-start | bytes 49160 | tf_op jit(solution)/shard_map/ppermute | solution.py:418
  13.8 67.3 %collective-permute-start.13 = (f32[2,2,8,128]{3,2,1,0:T(8,128)}, f32[2,2,8,128]{3,2,1,0:T(8,128)S(1)}, u32[]{:S(2)}, u32[]{:S(2)}) collective-permute-start(f32[2,2,8,128]{3,2,1,0:T(8,128)} %get-tuple-element.24), channel_id=1, source_target_pairs={{8,1},{9,2},{10,3},{11,4},{12,5},{13,6},{14,7},{16,9},{17,10},{18,... | collective-permute-start | bytes 49160 | tf_op jit(solution)/shard_map/ppermute | solution.py:418
  15.1 67.3 %collective-permute-start.10 = (f32[2,2,8,128]{3,2,1,0:T(8,128)}, f32[2,2,8,128]{3,2,1,0:T(8,128)}, u32[]{:S(2)}, u32[]{:S(2)}) collective-permute-start(f32[2,2,8,128]{3,2,1,0:T(8,128)} %get-tuple-element.26), channel_id=1, source_target_pairs={{1,8},{2,9},{3,10},{4,11},{5,12},{6,13},{7,14},{9,16},{10,17},{11,... | collective-permute-start | bytes 49160 | tf_op jit(solution)/shard_map/ppermute | solution.py:418
  18.0 17.3 %copy-start.13 = (s32[512,1]{0,1:T(1,128)}, s32[512,1]{0,1:T(1,128)S(1)}, u32[]{:S(2)}) copy-start(s32[512,1]{0,1:T(1,128)S(1)} %compare_select_fusion) | copy-start | bytes 6148
  23.7 18.5 %all-to-all-start = ((f32[16,1,128]{2,1,0:T(1,128)}), f32[16,1,128]{2,1,0:T(1,128)S(1)}, u32[]{:S(2)}, u32[]{:S(2)}) async-start(f32[16,1,128]{2,1,0:T(1,128)} %bitcast.13), calls=%async_computation | async-start | bytes 16384 | tf_op jit(solution)/shard_map/all_to_all | solution.py:473
  42.5 6.2 %collective-permute-start.16 = (f32[2,1024]{1,0:T(2,128)S(1)}, f32[2,1024]{1,0:T(2,128)S(1)}, u32[]{:S(2)}, u32[]{:S(2)}) collective-permute-start(f32[2,1024]{1,0:T(2,128)S(1)} %pad_maximum_fusion.4), channel_id=1, source_target_pairs={{0,1},{1,2},{2,3},{3,4},{4,5},{5,6},{6,7},{7,0},{8,9},{9,10},{10,1... | collective-permute-start | bytes 24584 | tf_op jit(solution)/shard_map/ppermute | solution.py:435
  48.7 3.7 %collective-permute-start.17 = (f32[2,1024]{1,0:T(2,128)S(1)}, f32[2,1024]{1,0:T(2,128)S(1)}, u32[]{:S(2)}, u32[]{:S(2)}) collective-permute-start(f32[2,1024]{1,0:T(2,128)S(1)} %pad_maximum_fusion.4), channel_id=1, source_target_pairs={{0,2},{1,3},{2,4},{3,5},{4,6},{5,7},{6,0},{7,1},{8,10},{9,11},{10,... | collective-permute-start | bytes 24584 | tf_op jit(solution)/shard_map/ppermute | solution.py:435
  52.4 4.9 %collective-permute-start.18 = (f32[2,1024]{1,0:T(2,128)S(1)}, f32[2,1024]{1,0:T(2,128)S(1)}, u32[]{:S(2)}, u32[]{:S(2)}) collective-permute-start(f32[2,1024]{1,0:T(2,128)S(1)} %pad_maximum_fusion.4), channel_id=1, source_target_pairs={{0,3},{1,4},{2,5},{3,6},{4,7},{5,0},{6,1},{7,2},{8,11},{9,12},{10,... | collective-permute-start | bytes 24584 | tf_op jit(solution)/shard_map/ppermute | solution.py:435
  57.3 4.0 %collective-permute-start.19 = (f32[2,1024]{1,0:T(2,128)S(1)}, f32[2,1024]{1,0:T(2,128)S(1)}, u32[]{:S(2)}, u32[]{:S(2)}) collective-permute-start(f32[2,1024]{1,0:T(2,128)S(1)} %pad_maximum_fusion.4), channel_id=1, source_target_pairs={{0,4},{1,5},{2,6},{3,7},{4,0},{5,1},{6,2},{7,3},{8,12},{9,13},{10,... | collective-permute-start | bytes 24584 | tf_op jit(solution)/shard_map/ppermute | solution.py:435
  61.4 3.7 %collective-permute-start.20 = (f32[2,1024]{1,0:T(2,128)S(1)}, f32[2,1024]{1,0:T(2,128)S(1)}, u32[]{:S(2)}, u32[]{:S(2)}) collective-permute-start(f32[2,1024]{1,0:T(2,128)S(1)} %pad_maximum_fusion.4), channel_id=1, source_target_pairs={{0,5},{1,6},{2,7},{3,0},{4,1},{5,2},{6,3},{7,4},{8,13},{9,14},{10,... | collective-permute-start | bytes 24584 | tf_op jit(solution)/shard_map/ppermute | solution.py:435
  65.1 2.5 collective-permute-start.21
  67.6 2.5 collective-permute-start.22
  70.1 44.8 %collective-permute-start.5 = (bf16[2,256,256]{2,1,0:T(8,128)(2,1)}, bf16[2,256,256]{2,1,0:T(8,128)(2,1)}, u32[]{:S(2)}, u32[]{:S(2)}) collective-permute-start(bf16[2,256,256]{2,1,0:T(8,128)(2,1)} %get-tuple-element.15), channel_id=1, source_target_pairs={{1,8},{2,9},{3,10},{4,11},{5,12},{6,13},{7,14},{9,16},{10,17},{11,... | collective-permute-start | bytes 786440 | tf_op jit(solution)/shard_map/ppermute | solution.py:418
  71.4 20.6 %copy-start.11 = (f32[2,2,8,128]{3,2,1,0:T(8,128)}, f32[2,2,8,128]{3,2,1,0:T(8,128)S(1)}, u32[]{:S(2)}) copy-start(f32[2,2,8,128]{3,2,1,0:T(8,128)S(1)} %collective-permute-done.15) | copy-start | bytes 49156
  71.4 25.0 %collective-permute-start.14 = (f32[2,4,8,128]{3,2,1,0:T(8,128)}, f32[2,4,8,128]{3,2,1,0:T(8,128)}, u32[]{:S(2)}, u32[]{:S(2)}) collective-permute-start(f32[2,4,8,128]{3,2,1,0:T(8,128)} %get-tuple-element.28), channel_id=1, source_target_pairs={{8,0},{9,1},{10,2},{11,3},{12,4},{13,5},{14,6},{15,7},{16,8},{17,9... | collective-permute-start | bytes 98312 | tf_op jit(solution)/shard_map/ppermute | solution.py:418
  81.1 10.8 %copy-start.12 = (f32[2,2,8,128]{3,2,1,0:T(8,128)}, f32[2,2,8,128]{3,2,1,0:T(8,128)S(1)}, u32[]{:S(2)}) copy-start(f32[2,2,8,128]{3,2,1,0:T(8,128)S(1)} %collective-permute-done.13) | copy-start | bytes 49156
  81.1 18.6 %collective-permute-start.12 = (f32[4,2,8,128]{3,2,1,0:T(8,128)}, f32[4,2,8,128]{3,2,1,0:T(8,128)}, u32[]{:S(2)}, u32[]{:S(2)}) collective-permute-start(f32[4,2,8,128]{3,2,1,0:T(8,128)} %get-tuple-element.30), channel_id=1, source_target_pairs={{1,0},{2,1},{3,2},{4,3},{5,4},{6,5},{7,6},{9,8},{10,9},{11,10},{12... | collective-permute-start | bytes 98312 | tf_op jit(solution)/shard_map/ppermute | solution.py:418
  82.4 11.7 %collective-permute-start.8 = (f32[2,2,8,128]{3,2,1,0:T(8,128)}, f32[2,2,8,128]{3,2,1,0:T(8,128)}, u32[]{:S(2)}, u32[]{:S(2)}) collective-permute-start(f32[2,2,8,128]{3,2,1,0:T(8,128)} %get-tuple-element.23), channel_id=1, source_target_pairs={{0,9},{1,10},{2,11},{3,12},{4,13},{5,14},{6,15},{8,17},{9,18},{10,... | collective-permute-start | bytes 49160 | tf_op jit(solution)/shard_map/ppermute | solution.py:418
  94.1 22.0 %collective-permute-start.6 = (bf16[2,256,256]{2,1,0:T(8,128)(2,1)}, bf16[2,256,256]{2,1,0:T(8,128)(2,1)S(1)}, u32[]{:S(2)}, u32[]{:S(2)}) collective-permute-start(bf16[2,256,256]{2,1,0:T(8,128)(2,1)} %get-tuple-element.14), channel_id=1, source_target_pairs={{8,1},{9,2},{10,3},{11,4},{12,5},{13,6},{14,7},{16,9},{17,10},{18,... | collective-permute-start | bytes 786440 | tf_op jit(solution)/shard_map/ppermute | solution.py:418
  96.4 10.5 %collective-permute-start.11 = (f32[4,2,8,128]{3,2,1,0:T(8,128)}, f32[4,2,8,128]{3,2,1,0:T(8,128)S(1)}, u32[]{:S(2)}, u32[]{:S(2)}) collective-permute-start(f32[4,2,8,128]{3,2,1,0:T(8,128)} %get-tuple-element.29), channel_id=1, source_target_pairs={{0,1},{1,2},{2,3},{3,4},{4,5},{5,6},{6,7},{8,9},{9,10},{10,11},{11... | collective-permute-start | bytes 98312 | tf_op jit(solution)/shard_map/ppermute | solution.py:418
  99.7 9.1 %collective-permute-start.9 = (f32[2,4,8,128]{3,2,1,0:T(8,128)}, f32[2,4,8,128]{3,2,1,0:T(8,128)S(1)}, u32[]{:S(2)}, u32[]{:S(2)}) collective-permute-start(f32[2,4,8,128]{3,2,1,0:T(8,128)} %get-tuple-element.27), channel_id=1, source_target_pairs={{0,8},{1,9},{2,10},{3,11},{4,12},{5,13},{6,14},{7,15},{8,16},{9,17... | collective-permute-start | bytes 98312 | tf_op jit(solution)/shard_map/ppermute | solution.py:418
  106.9 7.9 %copy-start.8 = (f32[4,2,8,128]{3,2,1,0:T(8,128)}, f32[4,2,8,128]{3,2,1,0:T(8,128)S(1)}, u32[]{:S(2)}) copy-start(f32[4,2,8,128]{3,2,1,0:T(8,128)S(1)} %collective-permute-done.11) | copy-start | bytes 98308
  106.9 106.9 %collective-permute-start = (bf16[2,256,512]{2,1,0:T(8,128)(2,1)}, bf16[2,256,512]{2,1,0:T(8,128)(2,1)}, u32[]{:S(2)}, u32[]{:S(2)}) collective-permute-start(bf16[2,256,512]{2,1,0:T(8,128)(2,1)} %get-tuple-element.20), channel_id=1, source_target_pairs={{0,8},{1,9},{2,10},{3,11},{4,12},{5,13},{6,14},{7,15},{8,16},{9,17... | collective-permute-start | bytes 1572872 | tf_op jit(solution)/shard_map/ppermute | solution.py:418
  108.8 6.0 %copy-start.9 = (f32[2,4,8,128]{3,2,1,0:T(8,128)}, f32[2,4,8,128]{3,2,1,0:T(8,128)S(1)}, u32[]{:S(2)}) copy-start(f32[2,4,8,128]{3,2,1,0:T(8,128)S(1)} %collective-permute-done.9) | copy-start | bytes 98308
  108.8 105.0 %collective-permute-start.1 = (bf16[2,256,512]{2,1,0:T(8,128)(2,1)}, bf16[2,256,512]{2,1,0:T(8,128)(2,1)}, u32[]{:S(2)}, u32[]{:S(2)}) collective-permute-start(bf16[2,256,512]{2,1,0:T(8,128)(2,1)} %get-tuple-element.19), channel_id=1, source_target_pairs={{8,0},{9,1},{10,2},{11,3},{12,4},{13,5},{14,6},{15,7},{16,8},{17,9... | collective-permute-start | bytes 1572872 | tf_op jit(solution)/shard_map/ppermute | solution.py:418
  112.0 101.8 %collective-permute-start.2 = (bf16[4,256,256]{2,1,0:T(8,128)(2,1)}, bf16[4,256,256]{2,1,0:T(8,128)(2,1)}, u32[]{:S(2)}, u32[]{:S(2)}) collective-permute-start(bf16[4,256,256]{2,1,0:T(8,128)(2,1)} %get-tuple-element.18), channel_id=1, source_target_pairs={{0,1},{1,2},{2,3},{3,4},{4,5},{5,6},{6,7},{8,9},{9,10},{10,11},{11... | collective-permute-start | bytes 1572872 | tf_op jit(solution)/shard_map/ppermute | solution.py:418
  114.8 99.0 %collective-permute-start.3 = (bf16[4,256,256]{2,1,0:T(8,128)(2,1)}, bf16[4,256,256]{2,1,0:T(8,128)(2,1)}, u32[]{:S(2)}, u32[]{:S(2)}) collective-permute-start(bf16[4,256,256]{2,1,0:T(8,128)(2,1)} %get-tuple-element.17), channel_id=1, source_target_pairs={{1,0},{2,1},{3,2},{4,3},{5,4},{6,5},{7,6},{9,8},{10,9},{11,10},{12... | collective-permute-start | bytes 1572872 | tf_op jit(solution)/shard_map/ppermute | solution.py:418
  116.2 0.7 copy-start.1
  116.9 96.9 %collective-permute-start.7 = (bf16[2,256,256]{2,1,0:T(8,128)(2,1)}, bf16[2,256,256]{2,1,0:T(8,128)(2,1)}, u32[]{:S(2)}, u32[]{:S(2)}) collective-permute-start(bf16[2,256,256]{2,1,0:T(8,128)(2,1)} %get-tuple-element.13), channel_id=1, source_target_pairs={{9,0},{10,1},{11,2},{12,3},{13,4},{14,5},{15,6},{17,8},{18,9},{19,... | collective-permute-start | bytes 786440 | tf_op jit(solution)/shard_map/ppermute | solution.py:418
  213.8 1.2 copy-start
  215.1 0.9 copy-start.2
  216.0 19.3 %copy-start.3 = (f32[2]{0:T(128)S(1)}, f32[2]{0:T(128)}, u32[]{:S(2)}) copy-start(f32[2]{0:T(128)} %pad_maximum_fusion.5.scale) | copy-start | bytes 28
  329.5 10.8 %copy-start.14 = (s32[512,1]{0,1:T(1,128)S(1)}, s32[512,1]{0,1:T(1,128)}, u32[]{:S(2)}) copy-start(s32[512,1]{0,1:T(1,128)} %copy-done.13) | copy-start | bytes 6148
  329.5 28.0 %all-to-all-start.2 = ((f32[16,64,256]{2,1,0:T(8,128)}), f32[16,64,256]{2,1,0:T(8,128)S(1)}, u32[]{:S(2)}, u32[]{:S(2)}) async-start(f32[16,64,256]{2,1,0:T(8,128)} %bitcast.60), calls=%async_computation.2 | async-start | bytes 2097152 | tf_op jit(solution)/shard_map/all_to_all | solution.py:496
